TPU v7x, 32 devices: a whole 2x2x4 slice. The times are simulated.
32 devices in a mesh: frame: 8 (over z, x), row: 4 (over y, core).
Axes of the slice: x: 2, y: 2, z: 4, core: 2. Of those that a mesh axis runs over, the one named last changes fastest.
Arguments:
- frames: float32 [64, 128, 2048], P('frame', 'row'), may hold values from -12 to 12
Outputs:
- estimate: float32 [128, 2048], P('row')
All inputs are finite; a program needn't handle non-finite values.
Results may differ from a plain program's by a relative error of at most 0.00002.
Values sent between devices are 32-bit elements; how exact they have to be, the bound alone decides.
No kernel may reach another device: no remote copies, remote signals or barrier semaphores. Data moves between devices by JAX's collectives and lax.ppermute only.
A program may use at most 64 MiB of HBM per device.

v0:
```python
import jax
import jax.numpy as jnp
from jax import lax
from jax.sharding import PartitionSpec as P

FRAMES = 64
ROUNDS = 3
GUIDE_EPS = 0.05
CAUCHY_SCALE = 0.5


def with_halo(x, sides, width):
    for axis, dim in sides:
        count, length = (lax.axis_size(axis), x.shape[dim])
        up = [(i, (i + 1) % count) for i in range(count - 1)]
        down = [(j, i) for i, j in up]
        last = lax.slice_in_dim(x, length - width, length, axis=dim)
        initial = lax.slice_in_dim(x, 0, width, axis=dim)
        before = lax.ppermute(last, axis, up)
        after = lax.ppermute(initial, axis, down)
        x = jnp.concatenate([before, x, after], axis=dim)
    return x


def row_sum(field):
    length = field.shape[-2] - 8
    total = field[..., 0:length, :]
    for offset in range(1, 9):
        total = total + field[..., offset : offset + length, :]
    return total


def col_sum(field):
    width = field.shape[-1]
    padded = jnp.pad(field, [(0, 0)] * (field.ndim - 1) + [(4, 4)])
    total = padded[..., 0:width]
    for offset in range(1, 9):
        total = total + padded[..., offset : offset + width]
    return total


def window_count(first, length, limit):
    place = first + jnp.arange(length, dtype=jnp.int32)
    lower = jnp.maximum(place - 4, 0)
    upper = jnp.minimum(place + 4, limit - 1)
    return jnp.maximum(upper - lower + 1, 1).astype(jnp.float32)


def smooth(padded_rows, area):
    return col_sum(row_sum(padded_rows)) / area


def shards(frames):
    local_rows = frames.shape[1]
    width = frames.shape[2]
    height = local_rows * lax.axis_size("row")
    start = lax.axis_index("row") * local_rows
    col_counts = window_count(0, width, width)
    estimate = lax.psum(jnp.sum(frames, axis=0), "frame") / FRAMES
    depth = 4
    padded_frames = with_halo(frames, (("row", 1),), 4)
    stat_rows = local_rows + 2 * depth - 8
    stat_first = start - depth + 4
    stat_area = window_count(stat_first, stat_rows, height)[:, None] * col_counts[None, :]
    out_area = window_count(start, local_rows, height)[:, None] * col_counts[None, :]
    for round_index in range(ROUNDS):
        padded_guide = with_halo(estimate, (("row", 0),), 4)
        mean_guide = smooth(padded_guide, stat_area)
        variance = smooth(padded_guide * padded_guide, stat_area) - mean_guide * mean_guide
        mean_frame = smooth(padded_frames, stat_area)
        cross = smooth(padded_guide[None] * padded_frames, stat_area)
        slope = (cross - mean_guide * mean_frame) / (variance + GUIDE_EPS)
        offset_term = mean_frame - slope * mean_guide
        stacked = with_halo(jnp.stack((slope, offset_term)), (("row", 2),), 4)
        slope_rows = stacked[0]
        offset_rows = stacked[1]
        filtered = smooth(slope_rows, out_area) * estimate[None] + smooth(offset_rows, out_area)
        gap = (filtered - estimate[None]) / CAUCHY_SCALE
        weight = 1.0 / (1.0 + gap * gap)
        weighted = jnp.sum(weight * frames, axis=0)
        total = jnp.sum(weight, axis=0)
        sums = lax.psum((weighted, total), "frame")
        estimate = sums[0] / sums[1]
    return estimate


def solution(mesh):
    return jax.shard_map(
        shards,
        mesh=mesh,
        in_specs=(P("frame", "row", None),),
        out_specs=P("row", None),
        check_vma=False,
    )
```

profile of v0, /device:TPU:0, one launch (start us, length us, event | category | flops | bytes accessed | tf_op | source)
XLA Modules:
  0.0 464.5 jit_solution(2341321879455873204)
XLA Ops:
  6.5 1.3 fusion.103
  7.8 2.4 collective-permute-start.2
  10.3 1.4 collective-permute-start.3
  11.7 1.8 constant_dynamic-update-slice_fusion.1
  13.5 2.4 collective-permute-done.3
  16.0 3.6 fusion.7
  19.7 75.9 %all-reduce.24.cloned.1.call-done = f32[32,2048]{1,0:T(8,128)} async-done(((f32[32,2048]{1,0:T(8,128)}), f32[32,2048]{1,0:T(8,128)}) %all-reduce.24.cloned.1.call-update) | async-done | bytes 262160 | tf_op jit(solution)/shard_map/psum | solution.py:59
  96.6 1.3 collective-permute-start
  97.9 1.3 collective-permute-start.1
  99.2 3.5 collective-permute-done.1
  103.2 2.5 slice_add_fusion.64
  106.1 1.9 fusion.74
  108.0 14.9 %subtract_bitcast_fusion.2 = (f32[1,8,32,2048]{3,2,1,0:T(8,128)S(1)}, f32[8,32,2048]{2,1,0:T(8,128)S(1)}, f32[8,32,2048]{2,1,0:T(8,128)}) fusion(f32[32,2048]{1,0:T(8,128)} %get-tuple-element.29, f32[32,2048]{1,0:T(8,128)S(1)} %get-tuple-element.28, f32[32,2048]{1,0:T(8,128)S(1)} %get-tuple-element.58, f32[8,32,2048]{2,1,0:T(8,128)} %slice_add_fusion.64, ...), kind=kLoop, calls=%fused_computation.150 | loop fusion | flops 12058624 | bytes 11272192 | tf_op jit(solution)/shard_map/stack | solution.py:74
  123.1 4.6 collective-permute-start.4
  127.7 1.6 collective-permute-start.5
  129.3 2.2 collective-permute-done.5
  132.9 1.5 slice_add_fusion.56
  134.5 1.5 slice_add_fusion.48
  136.1 9.7 %fusion.102 = (f32[32,2048]{1,0:T(8,128)}, f32[32,2048]{1,0:T(8,128)}) fusion(f32[8,32,2048]{2,1,0:T(8,128)S(1)} %copy-done, f32[8,32,2048]{2,1,0:T(8,128)S(1)} %slice_add_fusion.48, f32[32,2048]{1,0:T(8,128)S(1)} %broadcast_multiply_fusion.4, f32[32,2048]{1,0:T(8,128)S(1)} %get-tuple-element.58, f32[8,32,2048]{2,1,0:T(8,128)S(1)} %slice_add_fusion.56), kind=kLoop, calls=%fused_computation.343 | loop fusion | flops 14548992 | bytes 7340032 | tf_op jit(solution)/shard_map/reduce_sum | solution.py:81
  145.8 77.5 %all-reduce.30.cloned.1.call-done = (f32[32,2048]{1,0:T(8,128)}, f32[32,2048]{1,0:T(8,128)}) async-done(((f32[32,2048]{1,0:T(8,128)}, f32[32,2048]{1,0:T(8,128)}), (f32[32,2048]{1,0:T(8,128)}, f32[32,2048]{1,0:T(8,128)})) %all-reduce.30.cloned.1.call-update) | async-done | bytes 524304 | tf_op jit(solution)/shard_map/psum | solution.py:82
  224.5 1.3 collective-permute-start.6
  225.8 1.8 collective-permute-start.7
  227.6 3.0 collective-permute-done.7
  231.3 1.5 slice_add_fusion.40
  233.1 1.2 fusion.76
  234.3 4.5 subtract_bitcast_fusion.1
  239.0 4.6 collective-permute-start.8
  243.6 1.5 collective-permute-start.9
  245.1 2.3 collective-permute-done.9
  247.4 1.2 pad_maximum_fusion.1
  249.2 1.5 slice_add_fusion.32
  250.8 1.5 slice_add_fusion.24
  252.3 9.7 %fusion.101 = (f32[32,2048]{1,0:T(8,128)}, f32[32,2048]{1,0:T(8,128)}) fusion(f32[8,32,2048]{2,1,0:T(8,128)S(1)} %copy-done, f32[8,32,2048]{2,1,0:T(8,128)S(1)} %slice_add_fusion.24, f32[32,2048]{1,0:T(8,128)S(1)} %div.158, f32[32,2048]{1,0:T(8,128)S(1)} %get-tuple-element.58, f32[8,32,2048]{2,1,0:T(8,128)S(1)} %slice_add_fusion.32), kind=kLoop, calls=%fused_computation.342 | loop fusion | flops 14548992 | bytes 7340032 | tf_op jit(solution)/shard_map/reduce_sum | solution.py:81
  262.1 77.6 %all-reduce.28.cloned.1.call-done = (f32[32,2048]{1,0:T(8,128)}, f32[32,2048]{1,0:T(8,128)}) async-done(((f32[32,2048]{1,0:T(8,128)}, f32[32,2048]{1,0:T(8,128)}), (f32[32,2048]{1,0:T(8,128)}, f32[32,2048]{1,0:T(8,128)})) %all-reduce.28.cloned.1.call-update) | async-done | bytes 524304 | tf_op jit(solution)/shard_map/psum | solution.py:82
  340.8 1.3 collective-permute-start.10
  342.1 1.5 collective-permute-start.11
  343.6 3.3 collective-permute-done.11
  347.6 1.5 slice_add_fusion.16
  350.6 4.5 subtract_bitcast_fusion
  355.3 4.6 collective-permute-start.12
  359.9 1.5 collective-permute-start.13
  361.5 2.2 collective-permute-done.13
  363.7 1.2 pad_maximum_fusion.2
  365.5 1.5 slice_add_fusion.8
  367.1 1.5 slice_add_fusion
  368.6 9.7 %fusion.100 = (f32[32,2048]{1,0:T(8,128)}, f32[32,2048]{1,0:T(8,128)}) fusion(f32[8,32,2048]{2,1,0:T(8,128)S(1)} %copy-done, f32[8,32,2048]{2,1,0:T(8,128)S(1)} %slice_add_fusion, f32[32,2048]{1,0:T(8,128)S(1)} %div.168, f32[32,2048]{1,0:T(8,128)S(1)} %get-tuple-element.58, f32[8,32,2048]{2,1,0:T(8,128)S(1)} %slice_add_fusion.8), kind=kLoop, calls=%fused_computation.341 | loop fusion | flops 14548992 | bytes 7340032 | tf_op jit(solution)/shard_map/reduce_sum | solution.py:81
  378.3 77.7 %all-reduce.26.cloned.1.call-done = (f32[32,2048]{1,0:T(8,128)}, f32[32,2048]{1,0:T(8,128)}) async-done(((f32[32,2048]{1,0:T(8,128)}, f32[32,2048]{1,0:T(8,128)}), (f32[32,2048]{1,0:T(8,128)}, f32[32,2048]{1,0:T(8,128)})) %all-reduce.26.cloned.1.call-update) | async-done | bytes 524304 | tf_op jit(solution)/shard_map/psum | solution.py:82
  456.0 1.8 div.178
  (51 shorter events, 10.8 us)
Async XLA Ops:
  6.5 89.1 %all-reduce.24.cloned.1.call-start = ((), (), s32[]{:S(2)}) async-start(), calls=%async_computation | async-start | bytes 524288 | tf_op jit(solution)/shard_map/psum | solution.py:59
  7.8 8.2 %collective-permute-start.2 = (f32[8,4,2048]{2,1,0:T(4,128)S(1)}, f32[8,4,2048]{2,1,0:T(4,128)S(1)}, u32[]{:S(2)}, u32[]{:S(2)}) collective-permute-start(f32[8,4,2048]{2,1,0:T(4,128)S(1)} %get-tuple-element.44), channel_id=1, source_target_pairs={{0,1},{1,2},{2,3},{4,5},{5,6},{6,7},{8,9},{9,10},{10,11},{12,13},{... | collective-permute-start | bytes 786440 | tf_op jit(solution)/shard_map/ppermute | solution.py:19
  10.3 5.8 %copy-start = (f32[8,32,2048]{2,1,0:T(8,128)S(1)}, f32[8,32,2048]{2,1,0:T(8,128)}, u32[]{:S(2)}) copy-start(f32[8,32,2048]{2,1,0:T(8,128)} %param.1) | copy-start | bytes 6291460
  10.3 5.7 %collective-permute-start.3 = (f32[8,4,2048]{2,1,0:T(4,128)S(1)}, f32[8,4,2048]{2,1,0:T(4,128)S(1)}, u32[]{:S(2)}, u32[]{:S(2)}) collective-permute-start(f32[8,4,2048]{2,1,0:T(4,128)S(1)} %get-tuple-element.45), channel_id=1, source_target_pairs={{1,0},{2,1},{3,2},{5,4},{6,5},{7,6},{9,8},{10,9},{11,10},{13,12},{... | collective-permute-start | bytes 786440 | tf_op jit(solution)/shard_map/ppermute | solution.py:20
  19.7 203.7 %all-reduce.30.cloned.1.call-start = ((), (), s32[]{:S(2)}) async-start(), calls=%async_computation.3 | async-start | bytes 1048576 | tf_op jit(solution)/shard_map/psum | solution.py:82
  96.6 2.6 collective-permute-start
  97.9 4.8 %collective-permute-start.1 = (f32[4,2048]{1,0:T(4,128)S(1)}, f32[4,2048]{1,0:T(4,128)S(1)}, u32[]{:S(2)}, u32[]{:S(2)}) collective-permute-start(f32[4,2048]{1,0:T(4,128)S(1)} %get-tuple-element.57), channel_id=1, source_target_pairs={{1,0},{2,1},{3,2},{5,4},{6,5},{7,6},{9,8},{10,9},{11,10},{13,12},{... | collective-permute-start | bytes 98312 | tf_op jit(solution)/shard_map/ppermute | solution.py:20
  105.7 2.3 copy-start.3
  123.1 6.2 %collective-permute-start.4 = (f32[2,8,4,2048]{3,2,1,0:T(4,128)S(1)}, f32[2,8,4,2048]{3,2,1,0:T(4,128)S(1)}, u32[]{:S(2)}, u32[]{:S(2)}) collective-permute-start(f32[2,8,4,2048]{3,2,1,0:T(4,128)S(1)} %get-tuple-element.40), channel_id=1, source_target_pairs={{0,1},{1,2},{2,3},{4,5},{5,6},{6,7},{8,9},{9,10},{10,11},{12,13},{... | collective-permute-start | bytes 1572872 | tf_op jit(solution)/shard_map/ppermute | solution.py:19
  127.7 3.8 collective-permute-start.5
  145.8 193.9 %all-reduce.28.cloned.1.call-start = ((), (), s32[]{:S(2)}) async-start(), calls=%async_computation.2 | async-start | bytes 1048576 | tf_op jit(solution)/shard_map/psum | solution.py:82
  224.5 3.1 collective-permute-start.6
  225.8 4.8 %collective-permute-start.7 = (f32[4,2048]{1,0:T(4,128)S(1)}, f32[4,2048]{1,0:T(4,128)S(1)}, u32[]{:S(2)}, u32[]{:S(2)}) collective-permute-start(f32[4,2048]{1,0:T(4,128)S(1)} %get-tuple-element.55), channel_id=1, source_target_pairs={{1,0},{2,1},{3,2},{5,4},{6,5},{7,6},{9,8},{10,9},{11,10},{13,12},{... | collective-permute-start | bytes 98312 | tf_op jit(solution)/shard_map/ppermute | solution.py:20
  231.3 3.0 copy-start.1
  239.0 6.1 %collective-permute-start.8 = (f32[2,8,4,2048]{3,2,1,0:T(4,128)S(1)}, f32[2,8,4,2048]{3,2,1,0:T(4,128)S(1)}, u32[]{:S(2)}, u32[]{:S(2)}) collective-permute-start(f32[2,8,4,2048]{3,2,1,0:T(4,128)S(1)} %get-tuple-element.38), channel_id=1, source_target_pairs={{0,1},{1,2},{2,3},{4,5},{5,6},{6,7},{8,9},{9,10},{10,11},{12,13},{... | collective-permute-start | bytes 1572872 | tf_op jit(solution)/shard_map/ppermute | solution.py:19
  243.6 3.8 collective-permute-start.9
  262.0 193.9 %all-reduce.26.cloned.1.call-start = ((), (), s32[]{:S(2)}) async-start(), calls=%async_computation.1 | async-start | bytes 1048576 | tf_op jit(solution)/shard_map/psum | solution.py:82
  340.8 2.8 collective-permute-start.10
  342.1 4.8 %collective-permute-start.11 = (f32[4,2048]{1,0:T(4,128)S(1)}, f32[4,2048]{1,0:T(4,128)S(1)}, u32[]{:S(2)}, u32[]{:S(2)}) collective-permute-start(f32[4,2048]{1,0:T(4,128)S(1)} %get-tuple-element.53), channel_id=1, source_target_pairs={{1,0},{2,1},{3,2},{5,4},{6,5},{7,6},{9,8},{10,9},{11,10},{13,12},{... | collective-permute-start | bytes 98312 | tf_op jit(solution)/shard_map/ppermute | solution.py:20
  347.6 3.0 copy-start.2
  355.3 6.1 %collective-permute-start.12 = (f32[2,8,4,2048]{3,2,1,0:T(4,128)S(1)}, f32[2,8,4,2048]{3,2,1,0:T(4,128)S(1)}, u32[]{:S(2)}, u32[]{:S(2)}) collective-permute-start(f32[2,8,4,2048]{3,2,1,0:T(4,128)S(1)} %get-tuple-element.36), channel_id=1, source_target_pairs={{0,1},{1,2},{2,3},{4,5},{5,6},{6,7},{8,9},{9,10},{10,11},{12,13},{... | collective-permute-start | bytes 1572872 | tf_op jit(solution)/shard_map/ppermute | solution.py:19
  359.9 3.8 collective-permute-start.13
Sparse Core Ops, SparseCore 0:
  19.8 75.7 all-reduce.23
  145.9 77.4 all-reduce.29
  262.2 77.4 all-reduce.27
  378.4 77.4 all-reduce.25
where the time goes:
time: 472 us; the launch traced here: 465 us
  waiting for transfers between devices  328 us (69%)
  other arithmetic  87.1 us (18%)
  starting transfers between devices  30.7 us (7%)
  between operations  13.9 us (3%)
  local copies, waits for them, and re-layouts  5.12 us (1%)
    psum x3, waiting for transfers between devices, shards(): sums = lax.psum((weighted, total), 'frame')  233 us
    psum x1, waiting for transfers between devices, shards(): estimate = lax.psum(jnp.sum(frames, axis=0), 'frame') / FRAMES  75.9 us
    reduce_sum x3, other arithmetic, shards(): total = jnp.sum(weight, axis=0)  29.1 us
    another operation x3, other arithmetic, shards(): stacked = with_halo(jnp.stack((slope, offset_term)), (('row', 2),), 4)  23.9 us
    ppermute x7, starting transfers between devices, with_halo(): before = lax.ppermute(last, axis, up)  20 us
    add x15, other arithmetic, row_sum(): total = total + field[..., offset:offset + length, :]  19.8 us
    ppermute x7, waiting for transfers between devices, with_halo(): after = lax.ppermute(initial, axis, down)  18.9 us
    ppermute x7, starting transfers between devices, with_halo(): after = lax.ppermute(initial, axis, down)  10.6 us
  transfers between devices with their start and end apart: 18, of which 11 were waited for; matrix products, arithmetic and copies ran while one was open for 0% of the time, Pallas kernels for 0%

commit v1 on v0

--- a/solution.py
+++ b/solution.py
@@ -56,7 +56,7 @@
     height = local_rows * lax.axis_size("row")
     start = lax.axis_index("row") * local_rows
     col_counts = window_count(0, width, width)
-    estimate = lax.psum(jnp.sum(frames, axis=0), "frame") / FRAMES
+    estimate = jnp.sum(lax.all_gather(jnp.sum(frames, axis=0), "frame"), axis=0) / FRAMES
     depth = 4
     padded_frames = with_halo(frames, (("row", 1),), 4)
     stat_rows = local_rows + 2 * depth - 8

time: 472 us -> 450 us (0.953)
  waiting for transfers between devices: 328 us -> 305 us
    psum x1 -> x0, waiting for transfers between devices: 75.9 us -> none  [shards(): estimate = lax.psum(jnp.sum(frames, axis=0), 'frame') / FRAMES]
    all_gather x0 -> x1, waiting for transfers between devices: none -> 53.9 us  [shards(): lax.all_gather(jnp.sum(frames, axis=0), 'frame')]
where the time goes in v1:
time: 450 us; the launch traced here: 442 us
  waiting for transfers between devices  305 us (68%)
  other arithmetic  88 us (20%)
  starting transfers between devices  30.7 us (7%)
  between operations  13.9 us (3%)
  local copies, waits for them, and re-layouts  4.64 us (1%)
    psum x3, waiting for transfers between devices, shards(): sums = lax.psum((weighted, total), 'frame')  232 us
    all_gather x1, waiting for transfers between devices, shards(): lax.all_gather(jnp.sum(frames, axis=0), 'frame')  53.9 us
    reduce_sum x3, other arithmetic, shards(): total = jnp.sum(weight, axis=0)  29.1 us
    another operation x3, other arithmetic, shards(): stacked = with_halo(jnp.stack((slope, offset_term)), (('row', 2),), 4)  23.9 us
    ppermute x7, starting transfers between devices, with_halo(): before = lax.ppermute(last, axis, up)  20 us
    add x15, other arithmetic, row_sum(): total = total + field[..., offset:offset + length, :]  19.8 us
    ppermute x7, waiting for transfers between devices, with_halo(): after = lax.ppermute(initial, axis, down)  18.9 us
    ppermute x7, starting transfers between devices, with_halo(): after = lax.ppermute(initial, axis, down)  10.6 us
  transfers between devices with their start and end apart: 18, of which 11 were waited for; matrix products, arithmetic and copies ran while one was open for 0% of the time, Pallas kernels for 0%

profile of v1, /device:TPU:0, one launch (start us, length us, event | category | flops | bytes accessed | tf_op | source)
XLA Modules:
  0.0 442.3 jit_solution(17504944280405846789)
XLA Ops:
  6.5 1.3 fusion.103
  7.8 2.4 collective-permute-start.2
  10.3 1.4 collective-permute-start.3
  11.7 1.8 constant_dynamic-update-slice_fusion.1
  13.5 2.4 collective-permute-done.3
  16.0 3.6 fusion.7
  19.7 53.9 %all-gather.3.cloned.1.call-done = f32[256,2048]{1,0:T(8,128)} async-done(((f32[32,2048]{1,0:T(8,128)}), f32[256,2048]{1,0:T(8,128)}) %all-gather.3.cloned.1.call-update) | async-done | bytes 2097168 | tf_op jit(solution)/shard_map/all_gather | solution.py:59
  73.6 1.7 reduce_sum.73
  75.4 1.3 collective-permute-start
  76.7 1.3 collective-permute-start.1
  78.0 3.5 collective-permute-done.1
  82.0 2.5 slice_add_fusion.64
  84.9 1.9 fusion.74
  86.8 14.9 %subtract_bitcast_fusion.2 = (f32[1,8,32,2048]{3,2,1,0:T(8,128)S(1)}, f32[8,32,2048]{2,1,0:T(8,128)S(1)}, f32[8,32,2048]{2,1,0:T(8,128)}) fusion(f32[32,2048]{1,0:T(8,128)} %get-tuple-element.29, f32[32,2048]{1,0:T(8,128)S(1)} %get-tuple-element.28, f32[32,2048]{1,0:T(8,128)S(1)} %get-tuple-element.58, f32[8,32,2048]{2,1,0:T(8,128)} %slice_add_fusion.64, ...), kind=kLoop, calls=%fused_computation.150 | loop fusion | flops 12058624 | bytes 11272192 | tf_op jit(solution)/shard_map/stack | solution.py:74
  101.9 4.6 %collective-permute-start.4 = (f32[2,8,4,2048]{3,2,1,0:T(4,128)S(1)}, f32[2,8,4,2048]{3,2,1,0:T(4,128)S(1)}, u32[]{:S(2)}, u32[]{:S(2)}) collective-permute-start(f32[2,8,4,2048]{3,2,1,0:T(4,128)S(1)} %get-tuple-element.40), channel_id=1, source_target_pairs={{0,1},{1,2},{2,3},{4,5},{5,6},{6,7},{8,9},{9,10},{10,11},{12,13},{... | collective-permute-start | bytes 1572872 | tf_op jit(solution)/shard_map/ppermute | solution.py:19
  106.5 1.6 collective-permute-start.5
  108.1 2.2 collective-permute-done.5
  111.6 1.5 slice_add_fusion.56
  113.1 1.5 slice_add_fusion.48
  114.7 9.7 %fusion.102 = (f32[32,2048]{1,0:T(8,128)}, f32[32,2048]{1,0:T(8,128)}) fusion(f32[8,32,2048]{2,1,0:T(8,128)S(1)} %copy-done, f32[8,32,2048]{2,1,0:T(8,128)S(1)} %slice_add_fusion.48, f32[32,2048]{1,0:T(8,128)S(1)} %broadcast_multiply_fusion.4, f32[32,2048]{1,0:T(8,128)S(1)} %get-tuple-element.58, f32[8,32,2048]{2,1,0:T(8,128)S(1)} %slice_add_fusion.56), kind=kLoop, calls=%fused_computation.343 | loop fusion | flops 14548992 | bytes 7340032 | tf_op jit(solution)/shard_map/reduce_sum | solution.py:81
  124.4 76.9 %all-reduce.27.cloned.1.call-done = (f32[32,2048]{1,0:T(8,128)}, f32[32,2048]{1,0:T(8,128)}) async-done(((f32[32,2048]{1,0:T(8,128)}, f32[32,2048]{1,0:T(8,128)}), (f32[32,2048]{1,0:T(8,128)}, f32[32,2048]{1,0:T(8,128)})) %all-reduce.27.cloned.1.call-update) | async-done | bytes 524304 | tf_op jit(solution)/shard_map/psum | solution.py:82
  202.4 1.3 collective-permute-start.6
  203.7 1.8 collective-permute-start.7
  205.6 3.0 collective-permute-done.7
  209.2 1.5 slice_add_fusion.40
  212.2 4.5 %subtract_bitcast_fusion.1 = (f32[1,8,32,2048]{3,2,1,0:T(8,128)S(1)}, f32[8,32,2048]{2,1,0:T(8,128)S(1)}) fusion(f32[8,32,2048]{2,1,0:T(8,128)S(1)} %copy-done.1, f32[32,2048]{1,0:T(8,128)S(1)} %get-tuple-element.24, f32[32,2048]{1,0:T(8,128)S(1)} %get-tuple-element.23, f32[32,2048]{1,0:T(8,128)S(1)} %get-tuple-element.58, ...), kind=kLoop, calls=%fused_computation.131 | loop fusion | flops 7340032 | bytes 9175040 | tf_op jit(solution)/shard_map/stack | solution.py:74
  217.0 4.6 %collective-permute-start.8 = (f32[2,8,4,2048]{3,2,1,0:T(4,128)S(1)}, f32[2,8,4,2048]{3,2,1,0:T(4,128)S(1)}, u32[]{:S(2)}, u32[]{:S(2)}) collective-permute-start(f32[2,8,4,2048]{3,2,1,0:T(4,128)S(1)} %get-tuple-element.38), channel_id=1, source_target_pairs={{0,1},{1,2},{2,3},{4,5},{5,6},{6,7},{8,9},{9,10},{10,11},{12,13},{... | collective-permute-start | bytes 1572872 | tf_op jit(solution)/shard_map/ppermute | solution.py:19
  221.6 1.5 collective-permute-start.9
  223.1 2.3 collective-permute-done.9
  225.4 1.2 pad_maximum_fusion.1
  227.0 1.5 slice_add_fusion.32
  228.6 1.5 slice_add_fusion.24
  230.1 9.7 %fusion.101 = (f32[32,2048]{1,0:T(8,128)}, f32[32,2048]{1,0:T(8,128)}) fusion(f32[8,32,2048]{2,1,0:T(8,128)S(1)} %copy-done, f32[8,32,2048]{2,1,0:T(8,128)S(1)} %slice_add_fusion.24, f32[32,2048]{1,0:T(8,128)S(1)} %div.158, f32[32,2048]{1,0:T(8,128)S(1)} %get-tuple-element.58, f32[8,32,2048]{2,1,0:T(8,128)S(1)} %slice_add_fusion.32), kind=kLoop, calls=%fused_computation.342 | loop fusion | flops 14548992 | bytes 7340032 | tf_op jit(solution)/shard_map/reduce_sum | solution.py:81
  239.9 77.6 %all-reduce.25.cloned.1.call-done = (f32[32,2048]{1,0:T(8,128)}, f32[32,2048]{1,0:T(8,128)}) async-done(((f32[32,2048]{1,0:T(8,128)}, f32[32,2048]{1,0:T(8,128)}), (f32[32,2048]{1,0:T(8,128)}, f32[32,2048]{1,0:T(8,128)})) %all-reduce.25.cloned.1.call-update) | async-done | bytes 524304 | tf_op jit(solution)/shard_map/psum | solution.py:82
  318.6 1.3 collective-permute-start.10
  319.9 1.5 collective-permute-start.11
  321.4 3.3 collective-permute-done.11
  325.4 1.5 slice_add_fusion.16
  328.4 4.5 %subtract_bitcast_fusion = (f32[1,8,32,2048]{3,2,1,0:T(8,128)S(1)}, f32[8,32,2048]{2,1,0:T(8,128)S(1)}) fusion(f32[8,32,2048]{2,1,0:T(8,128)S(1)} %copy-done.2, f32[32,2048]{1,0:T(8,128)S(1)} %get-tuple-element.20, f32[32,2048]{1,0:T(8,128)S(1)} %get-tuple-element.19, f32[32,2048]{1,0:T(8,128)S(1)} %get-tuple-element.58, f32[8,32,2048]{2,1,0:T(8,128)S(1)} %slice_add_fusion.16), kind=kLoop, calls=%fused_computation.112 | loop fusion | flops 7340032 | bytes 9175040 | tf_op jit(solution)/shard_map/stack | solution.py:74
  333.2 4.6 %collective-permute-start.12 = (f32[2,8,4,2048]{3,2,1,0:T(4,128)S(1)}, f32[2,8,4,2048]{3,2,1,0:T(4,128)S(1)}, u32[]{:S(2)}, u32[]{:S(2)}) collective-permute-start(f32[2,8,4,2048]{3,2,1,0:T(4,128)S(1)} %get-tuple-element.36), channel_id=1, source_target_pairs={{0,1},{1,2},{2,3},{4,5},{5,6},{6,7},{8,9},{9,10},{10,11},{12,13},{... | collective-permute-start | bytes 1572872 | tf_op jit(solution)/shard_map/ppermute | solution.py:19
  337.8 1.5 collective-permute-start.13
  339.4 2.2 collective-permute-done.13
  341.6 1.2 pad_maximum_fusion.2
  343.2 1.5 slice_add_fusion.8
  344.8 1.5 slice_add_fusion
  346.3 9.7 %fusion.100 = (f32[32,2048]{1,0:T(8,128)}, f32[32,2048]{1,0:T(8,128)}) fusion(f32[8,32,2048]{2,1,0:T(8,128)S(1)} %copy-done, f32[8,32,2048]{2,1,0:T(8,128)S(1)} %slice_add_fusion, f32[32,2048]{1,0:T(8,128)S(1)} %div.168, f32[32,2048]{1,0:T(8,128)S(1)} %get-tuple-element.58, f32[8,32,2048]{2,1,0:T(8,128)S(1)} %slice_add_fusion.8), kind=kLoop, calls=%fused_computation.341 | loop fusion | flops 14548992 | bytes 7340032 | tf_op jit(solution)/shard_map/reduce_sum | solution.py:81
  356.0 77.7 %all-reduce.23.cloned.1.call-done = (f32[32,2048]{1,0:T(8,128)}, f32[32,2048]{1,0:T(8,128)}) async-done(((f32[32,2048]{1,0:T(8,128)}, f32[32,2048]{1,0:T(8,128)}), (f32[32,2048]{1,0:T(8,128)}, f32[32,2048]{1,0:T(8,128)})) %all-reduce.23.cloned.1.call-update) | async-done | bytes 524304 | tf_op jit(solution)/shard_map/psum | solution.py:82
  433.7 1.8 div.178
  (52 shorter events, 10.6 us)
Async XLA Ops:
  6.5 67.1 %all-gather.3.cloned.1.call-start = ((), (), s32[]{:S(2)}) async-start(), calls=%async_computation | async-start | bytes 2359296 | tf_op jit(solution)/shard_map/all_gather | solution.py:59
  7.8 8.2 %collective-permute-start.2 = (f32[8,4,2048]{2,1,0:T(4,128)S(1)}, f32[8,4,2048]{2,1,0:T(4,128)S(1)}, u32[]{:S(2)}, u32[]{:S(2)}) collective-permute-start(f32[8,4,2048]{2,1,0:T(4,128)S(1)} %get-tuple-element.44), channel_id=1, source_target_pairs={{0,1},{1,2},{2,3},{4,5},{5,6},{6,7},{8,9},{9,10},{10,11},{12,13},{... | collective-permute-start | bytes 786440 | tf_op jit(solution)/shard_map/ppermute | solution.py:19
  10.3 5.8 %copy-start = (f32[8,32,2048]{2,1,0:T(8,128)S(1)}, f32[8,32,2048]{2,1,0:T(8,128)}, u32[]{:S(2)}) copy-start(f32[8,32,2048]{2,1,0:T(8,128)} %param.1) | copy-start | bytes 6291460
  10.3 5.7 %collective-permute-start.3 = (f32[8,4,2048]{2,1,0:T(4,128)S(1)}, f32[8,4,2048]{2,1,0:T(4,128)S(1)}, u32[]{:S(2)}, u32[]{:S(2)}) collective-permute-start(f32[8,4,2048]{2,1,0:T(4,128)S(1)} %get-tuple-element.45), channel_id=1, source_target_pairs={{1,0},{2,1},{3,2},{5,4},{6,5},{7,6},{9,8},{10,9},{11,10},{13,12},{... | collective-permute-start | bytes 786440 | tf_op jit(solution)/shard_map/ppermute | solution.py:20
  19.7 181.6 %all-reduce.27.cloned.1.call-start = ((), (), s32[]{:S(2)}) async-start(), calls=%async_computation.3 | async-start | bytes 1048576 | tf_op jit(solution)/shard_map/psum | solution.py:82
  75.4 2.6 collective-permute-start
  76.7 4.8 %collective-permute-start.1 = (f32[4,2048]{1,0:T(4,128)S(1)}, f32[4,2048]{1,0:T(4,128)S(1)}, u32[]{:S(2)}, u32[]{:S(2)}) collective-permute-start(f32[4,2048]{1,0:T(4,128)S(1)} %get-tuple-element.57), channel_id=1, source_target_pairs={{1,0},{2,1},{3,2},{5,4},{6,5},{7,6},{9,8},{10,9},{11,10},{13,12},{... | collective-permute-start | bytes 98312 | tf_op jit(solution)/shard_map/ppermute | solution.py:20
  84.5 2.3 copy-start.3
  101.9 6.2 %collective-permute-start.4 = (f32[2,8,4,2048]{3,2,1,0:T(4,128)S(1)}, f32[2,8,4,2048]{3,2,1,0:T(4,128)S(1)}, u32[]{:S(2)}, u32[]{:S(2)}) collective-permute-start(f32[2,8,4,2048]{3,2,1,0:T(4,128)S(1)} %get-tuple-element.40), channel_id=1, source_target_pairs={{0,1},{1,2},{2,3},{4,5},{5,6},{6,7},{8,9},{9,10},{10,11},{12,13},{... | collective-permute-start | bytes 1572872 | tf_op jit(solution)/shard_map/ppermute | solution.py:19
  106.5 3.8 collective-permute-start.5
  124.4 193.1 %all-reduce.25.cloned.1.call-start = ((), (), s32[]{:S(2)}) async-start(), calls=%async_computation.2 | async-start | bytes 1048576 | tf_op jit(solution)/shard_map/psum | solution.py:82
  202.4 3.1 collective-permute-start.6
  203.7 4.8 %collective-permute-start.7 = (f32[4,2048]{1,0:T(4,128)S(1)}, f32[4,2048]{1,0:T(4,128)S(1)}, u32[]{:S(2)}, u32[]{:S(2)}) collective-permute-start(f32[4,2048]{1,0:T(4,128)S(1)} %get-tuple-element.55), channel_id=1, source_target_pairs={{1,0},{2,1},{3,2},{5,4},{6,5},{7,6},{9,8},{10,9},{11,10},{13,12},{... | collective-permute-start | bytes 98312 | tf_op jit(solution)/shard_map/ppermute | solution.py:20
  209.2 3.0 copy-start.1
  217.0 6.1 %collective-permute-start.8 = (f32[2,8,4,2048]{3,2,1,0:T(4,128)S(1)}, f32[2,8,4,2048]{3,2,1,0:T(4,128)S(1)}, u32[]{:S(2)}, u32[]{:S(2)}) collective-permute-start(f32[2,8,4,2048]{3,2,1,0:T(4,128)S(1)} %get-tuple-element.38), channel_id=1, source_target_pairs={{0,1},{1,2},{2,3},{4,5},{5,6},{6,7},{8,9},{9,10},{10,11},{12,13},{... | collective-permute-start | bytes 1572872 | tf_op jit(solution)/shard_map/ppermute | solution.py:19
  221.6 3.8 collective-permute-start.9
  239.9 193.8 %all-reduce.23.cloned.1.call-start = ((), (), s32[]{:S(2)}) async-start(), calls=%async_computation.1 | async-start | bytes 1048576 | tf_op jit(solution)/shard_map/psum | solution.py:82
  318.6 2.8 collective-permute-start.10
  319.9 4.8 %collective-permute-start.11 = (f32[4,2048]{1,0:T(4,128)S(1)}, f32[4,2048]{1,0:T(4,128)S(1)}, u32[]{:S(2)}, u32[]{:S(2)}) collective-permute-start(f32[4,2048]{1,0:T(4,128)S(1)} %get-tuple-element.53), channel_id=1, source_target_pairs={{1,0},{2,1},{3,2},{5,4},{6,5},{7,6},{9,8},{10,9},{11,10},{13,12},{... | collective-permute-start | bytes 98312 | tf_op jit(solution)/shard_map/ppermute | solution.py:20
  325.4 3.0 copy-start.2
  333.2 6.1 %collective-permute-start.12 = (f32[2,8,4,2048]{3,2,1,0:T(4,128)S(1)}, f32[2,8,4,2048]{3,2,1,0:T(4,128)S(1)}, u32[]{:S(2)}, u32[]{:S(2)}) collective-permute-start(f32[2,8,4,2048]{3,2,1,0:T(4,128)S(1)} %get-tuple-element.36), channel_id=1, source_target_pairs={{0,1},{1,2},{2,3},{4,5},{5,6},{6,7},{8,9},{9,10},{10,11},{12,13},{... | collective-permute-start | bytes 1572872 | tf_op jit(solution)/shard_map/ppermute | solution.py:19
  337.8 3.8 collective-permute-start.13
Sparse Core Ops, SparseCore 0:
  19.8 53.7 all-gather.2
  124.5 76.7 all-reduce.26
  240.0 77.4 all-reduce.24
  356.2 77.4 all-reduce.22
